TPU v7x, 256 devices: a whole 4x4x8 slice. The times are simulated.
256 devices in a mesh: grp: 8 (over y, core), sub: 32 (over x, z).
Axes of the slice: x: 4, y: 4, z: 8, core: 2. Of those that a mesh axis runs over, the one named last changes fastest.
Arguments:
- right_side: float32 [65536, 2048], P(('grp', 'sub'))
- schur: bfloat16 [131072, 512], P(('grp', 'sub'))
- inv_factor: bfloat16 [131072, 512], P(('grp', 'sub'))
- coarse_inverse: float32 [2048, 256], P('grp')
- primal_index: int32 [256, 8], P(('grp', 'sub')), may hold values from 0 to 255
- phase: int32 [65536], P(('grp', 'sub')), may hold values from 0 to 3
- phase_coef: float32 [4], replicated, may hold values from 0.5 to 4
Outputs:
- solution: float32 [65536, 2048], P(('grp', 'sub'))
- residual: float32 [65536, 2048], P(('grp', 'sub'))
All inputs are finite; a program needn't handle non-finite values.
Results may differ from a plain program's by a relative error of at most 0.0056.
Values may be sent and summed in bfloat16 or wider, within the bound.
A program may use at most 64 MiB of HBM per device.

v0:
```python
import jax
import jax.numpy as jnp
from jax import lax
from jax.sharding import PartitionSpec as P


def shifted(value, axis, steps):
    count = lax.axis_size(axis)
    pairs = [(source, (source + steps) % count) for source in range(count)]
    return lax.ppermute(value, axis, pairs)


def transposed(matrix, operand):
    return lax.dot_general(
        matrix, operand, (((0,), (0,)), ((), ())), preferred_element_type=jnp.float32
    )


def body(right_side, schur, inv_factor, coarse_inverse, primal_index, phase, phase_coef):
    highest = lax.Precision.HIGHEST
    face_rows = right_side.shape[0]
    columns = jnp.arange(face_rows, dtype=jnp.int32)
    onehot = (primal_index[0][:, None] == columns[None, :]).astype(jnp.float32)
    primal_count = onehot.shape[0]
    resid_b = right_side.astype(jnp.bfloat16)
    left_resid = shifted(resid_b, "sub", 1)
    local_resid = jnp.concatenate([left_resid, resid_b], axis=0)
    first = jnp.dot(inv_factor, local_resid, preferred_element_type=jnp.float32).astype(
        jnp.bfloat16
    )
    second = transposed(inv_factor, first).astype(jnp.bfloat16)
    upper = second[:face_rows]
    from_right = shifted(upper, "sub", -1)
    lower = second[face_rows:]
    local_part = lower.astype(jnp.float32) + from_right.astype(jnp.float32)
    own_primal = jnp.dot(onehot, right_side, precision=highest)
    position = lax.axis_index("sub")
    group_primal = lax.all_gather(own_primal, "sub", axis=0, tiled=True)
    my_rows = lax.dynamic_slice_in_dim(coarse_inverse, position * primal_count, primal_count, 0)
    solved = jnp.dot(my_rows, group_primal, precision=highest)
    summed = lax.psum(solved, "grp")
    correction = solved + summed / lax.axis_size("grp")
    scattered = lax.dot_general(onehot, correction, (((0,), (0,)), ((), ())), precision=highest)
    direction = 0.5 * local_part + scattered
    dir_b = direction.astype(jnp.bfloat16)
    rz_part = jnp.sum(right_side * direction, axis=0)
    left_dir = shifted(dir_b, "sub", 1)
    image = jnp.dot(
        schur, jnp.concatenate([left_dir, dir_b], axis=0), preferred_element_type=jnp.float32
    ).astype(jnp.bfloat16)
    image_up = image[:face_rows]
    image_right = shifted(image_up, "sub", -1)
    image_low = image[face_rows:]
    phase_table = (
        phase[:, None] == jnp.arange(phase_coef.shape[0], dtype=jnp.int32)[None, :]
    ).astype(jnp.float32)
    coef_rows = jnp.dot(phase_table, phase_coef, precision=highest)
    dir_f = dir_b.astype(jnp.float32)
    qvec = (
        image_low.astype(jnp.float32) + image_right.astype(jnp.float32) + coef_rows[:, None] * dir_f
    )
    pq_part = jnp.sum(dir_f * qvec, axis=0)
    rz_total, pq_total = lax.psum((rz_part, pq_part), ("grp", "sub"))
    alpha = rz_total / pq_total
    return (alpha * dir_f, right_side - alpha * qvec)


def solution(mesh):
    in_specs = (
        P(("grp", "sub"), None),
        P(("grp", "sub"), None),
        P(("grp", "sub"), None),
        P("grp", None),
        P(("grp", "sub"), None),
        P(("grp", "sub")),
        P(),
    )
    out_specs = (P(("grp", "sub"), None), P(("grp", "sub"), None))
    return jax.shard_map(body, mesh=mesh, in_specs=in_specs, out_specs=out_specs, check_vma=False)
```

profile of v0, /device:TPU:1, one launch (start us, length us, event | category | flops | bytes accessed | tf_op | source)
XLA Modules:
  0.0 310.6 jit_solution(18175832615231809562)
XLA Ops:
  7.2 3.2 %fusion.21 = f32[8,2048]{1,0:T(8,128)} fusion(f32[256,2048]{1,0:T(8,128)} %param.7, s32[8]{0:T(128)} %bitcast.16), kind=kOutput, calls=%fused_computation.30 | convolution fusion | flops 50333696 | bytes 2162720 | tf_op jit(solution)/shard_map/dot_general | solution.py:36
  10.5 0.1 convert_element_type.39
  10.6 1.0 copy-done.6
  11.6 2.5 collective-permute-start
  14.1 30.4 %collective-permute-done = bf16[256,2048]{1,0:T(8,128)(2,1)} collective-permute-done((bf16[256,2048]{1,0:T(8,128)(2,1)S(1)}, bf16[256,2048]{1,0:T(8,128)(2,1)}, u32[]{:S(2)}, u32[]{:S(2)}) %collective-permute-start) | collective-permute-done | bytes 1048608 | tf_op jit(solution)/shard_map/ppermute | solution.py:10
  44.5 5.3 %fusion = bf16[512,2048]{1,0:T(8,128)(2,1)} fusion(bf16[512,512]{1,0:T(8,128)(2,1)S(1)} %copy-done, bf16[256,2048]{1,0:T(8,128)(2,1)} %copy-done.6, bf16[256,2048]{1,0:T(8,128)(2,1)} %collective-permute-done), kind=kOutput, calls=%fused_computation.6 | convolution fusion | flops 2153775104 | bytes 4718592 | tf_op jit(solution)/shard_map/dot_general | solution.py:14
  49.8 2.3 slice.17
  52.1 1.3 collective-permute-start.1
  53.4 39.7 %all-gather.2.cloned.1.call-done = f32[256,2048]{1,0:T(8,128)} async-done(((f32[8,2048]{1,0:T(8,128)}), f32[256,2048]{1,0:T(8,128)}) %all-gather.2.cloned.1.call-update) | async-done | bytes 2097168 | tf_op jit(solution)/shard_map/all_gather | solution.py:38
  93.1 3.3 %fusion.19 = f32[8,2048]{1,0:T(8,128)} fusion(f32[256,2048]{1,0:T(8,128)} %all-gather.2.cloned.1.call-done, f32[256,256]{1,0:T(8,128)} %param.10, s32[]{:T(128)S(6)} %select_n.3), kind=kOutput, calls=%fused_computation.27 | convolution fusion | flops 50331648 | bytes 2170884 | tf_op jit(solution)/shard_map/dot_general | solution.py:40
  96.4 65.5 %all-reduce.3.cloned.1.call-done = f32[8,2048]{1,0:T(8,128)} async-done(((f32[8,2048]{1,0:T(8,128)}), f32[8,2048]{1,0:T(8,128)}) %all-reduce.3.cloned.1.call-update) | async-done | bytes 65552 | tf_op jit(solution)/shard_map/psum | solution.py:41
  162.0 2.1 fusion.15
  164.1 1.9 multiply_reduce_fusion
  166.0 1.2 collective-permute-start.2
  167.2 24.4 %collective-permute-done.2 = bf16[256,2048]{1,0:T(8,128)(2,1)S(1)} collective-permute-done((bf16[256,2048]{1,0:T(8,128)(2,1)S(1)}, bf16[256,2048]{1,0:T(8,128)(2,1)S(1)}, u32[]{:S(2)}, u32[]{:S(2)}) %collective-permute-start.2) | collective-permute-done | bytes 1048608 | tf_op jit(solution)/shard_map/ppermute | solution.py:10
  191.7 1.3 fusion.1
  193.0 0.1 slice.19
  193.1 1.3 collective-permute-start.3
  194.4 0.2 fusion.13
  194.5 19.8 %collective-permute-done.3 = bf16[256,2048]{1,0:T(8,128)(2,1)S(1)} collective-permute-done((bf16[256,2048]{1,0:T(8,128)(2,1)S(1)}, bf16[256,2048]{1,0:T(8,128)(2,1)S(1)}, u32[]{:S(2)}, u32[]{:S(2)}) %collective-permute-start.3) | collective-permute-done | bytes 1048608 | tf_op jit(solution)/shard_map/ppermute | solution.py:10
  214.3 0.7 fusion.3
  215.0 0.3 copy-done.4
  215.3 83.7 %all-reduce = (f32[2048]{0:T(1024)S(1)}, f32[2048]{0:T(1024)S(1)}) all-reduce(f32[2048]{0:T(1024)S(1)} %get-tuple-element.4, f32[2048]{0:T(1024)S(1)} %fusion.3), channel_id=1, replica_groups=mesh['grp'=8,'sub'=32] {'grp','sub'}, use_global_device_ids=true, to_apply=%region_2.0 | all-reduce | flops 4096 | bytes 32768 | tf_op jit(solution)/shard_map/psum | solution.py:63
  299.0 4.8 %multiply_subtract_fusion = (f32[256,2048]{1,0:T(8,128)}, f32[256,2048]{1,0:T(8,128)}) fusion(f32[256,2048]{1,0:T(8,128)S(1)} %copy-done.1, bf16[256,2048]{1,0:T(8,128)(2,1)} %copy-done.2, bf16[256,2048]{1,0:T(8,128)(2,1)} %copy-done.4, f32[2048]{0:T(1024)S(1)} %div.11, f32[256]{0:T(256)S(1)} %bitcast.15, bf16[512,2048]{1,0:T(8,128)(2,1)} %copy-done.3), kind=kLoop, calls=%fused_computation.16 | loop fusion | flops 4718592 | bytes 9446400 | tf_op jit(solution)/shard_map/sub | solution.py:65
  (26 shorter events, 0.2 us)
Async XLA Ops:
  7.2 37.3 %copy-start = (bf16[512,512]{1,0:T(8,128)(2,1)S(1)}, bf16[512,512]{1,0:T(8,128)(2,1)}, u32[]{:S(2)}) copy-start(bf16[512,512]{1,0:T(8,128)(2,1)} %param.9) | copy-start | bytes 1572868
  7.2 3.3 %copy-start.1 = (f32[256,2048]{1,0:T(8,128)S(1)}, f32[256,2048]{1,0:T(8,128)}, u32[]{:S(2)}) copy-start(f32[256,2048]{1,0:T(8,128)} %param.7) | copy-start | bytes 6291460
  7.2 85.9 %all-gather.2.cloned.1.call-start = ((), (), s32[]{:S(2)}) async-start(), calls=%async_computation | async-start | bytes 2162688 | tf_op jit(solution)/shard_map/all_gather | solution.py:38
  10.4 151.5 %all-reduce.3.cloned.1.call-start = ((), (), s32[]{:S(2)}) async-start(), calls=%async_computation.1 | async-start | bytes 131072 | tf_op jit(solution)/shard_map/psum | solution.py:41
  10.6 1.0 copy-start.6
  11.6 32.9 %collective-permute-start = (bf16[256,2048]{1,0:T(8,128)(2,1)S(1)}, bf16[256,2048]{1,0:T(8,128)(2,1)}, u32[]{:S(2)}, u32[]{:S(2)}) collective-permute-start(bf16[256,2048]{1,0:T(8,128)(2,1)S(1)} %convert_element_type.39), channel_id=1, source_target_pairs={{0,1},{1,2},{2,3},{3,4},{4,5},{5,6},{6,7},{7,8},{8,9},{9,10},{10,1... | collective-permute-start | bytes 3145736 | tf_op jit(solution)/shard_map/ppermute | solution.py:10
  49.8 112.2 %copy-start.7 = (s32[1,8]{1,0:T(1,128)S(1)}, s32[1,8]{1,0:T(1,128)}, u32[]{:S(2)}) copy-start(s32[1,8]{1,0:T(1,128)} %param.11) | copy-start | bytes 100
  52.1 112.0 %collective-permute-start.1 = (bf16[256,2048]{1,0:T(8,128)(2,1)}, bf16[256,2048]{1,0:T(8,128)(2,1)}, u32[]{:S(2)}, u32[]{:S(2)}) collective-permute-start(bf16[256,2048]{1,0:T(8,128)(2,1)} %slice.17), channel_id=1, source_target_pairs={{0,31},{1,0},{2,1},{3,2},{4,3},{5,4},{6,5},{7,6},{8,7},{9,8},{10,9... | collective-permute-start | bytes 3145736 | tf_op jit(solution)/shard_map/ppermute | solution.py:10
  161.9 2.1 copy-start.5
  164.1 27.6 %copy-start.8 = (bf16[512,512]{1,0:T(8,128)(2,1)S(1)}, bf16[512,512]{1,0:T(8,128)(2,1)}, u32[]{:S(2)}) copy-start(bf16[512,512]{1,0:T(8,128)(2,1)} %param.8) | copy-start | bytes 1572868
  166.0 48.3 %copy-start.2 = (bf16[256,2048]{1,0:T(8,128)(2,1)}, bf16[256,2048]{1,0:T(8,128)(2,1)S(1)}, u32[]{:S(2)}) copy-start(bf16[256,2048]{1,0:T(8,128)(2,1)S(1)} %get-tuple-element.5) | copy-start | bytes 3145732
  166.0 25.7 %collective-permute-start.2 = (bf16[256,2048]{1,0:T(8,128)(2,1)S(1)}, bf16[256,2048]{1,0:T(8,128)(2,1)S(1)}, u32[]{:S(2)}, u32[]{:S(2)}) collective-permute-start(bf16[256,2048]{1,0:T(8,128)(2,1)S(1)} %get-tuple-element.5), channel_id=1, source_target_pairs={{0,1},{1,2},{2,3},{3,4},{4,5},{5,6},{6,7},{7,8},{8,9},{9,10},{10,1... | collective-permute-start | bytes 3145736 | tf_op jit(solution)/shard_map/ppermute | solution.py:10
  192.9 22.1 %copy-start.3 = (bf16[512,2048]{1,0:T(8,128)(2,1)}, bf16[512,2048]{1,0:T(8,128)(2,1)S(1)}, u32[]{:S(2)}) copy-start(bf16[512,2048]{1,0:T(8,128)(2,1)S(1)} %fusion.1) | copy-start | bytes 6291460
  193.0 1.4 copy-start.9
  193.0 1.4 copy-start.10
  193.1 21.2 %collective-permute-start.3 = (bf16[256,2048]{1,0:T(8,128)(2,1)S(1)}, bf16[256,2048]{1,0:T(8,128)(2,1)S(1)}, u32[]{:S(2)}, u32[]{:S(2)}) collective-permute-start(bf16[256,2048]{1,0:T(8,128)(2,1)S(1)} %slice.19), channel_id=1, source_target_pairs={{0,31},{1,0},{2,1},{3,2},{4,3},{5,4},{6,5},{7,6},{8,7},{9,8},{10,9... | collective-permute-start | bytes 3145736 | tf_op jit(solution)/shard_map/ppermute | solution.py:10
  214.3 1.0 copy-start.4
Sparse Core Ops, SparseCore 0:
  10.6 82.4 all-gather.1
  96.6 65.3 all-reduce.2
where the time goes:
time: 311 us
  waiting for transfers between devices  180 us (58%)
  blocking collectives  83.7 us (27%)
  matrix products  15.3 us (5%)
  between operations  14.2 us (5%)
  other arithmetic  7.52 us (2%)
  starting transfers between devices  6.3 us (2%)
  local copies, waits for them, and re-layouts  3.72 us (1%)
    psum x1, blocking collectives, body(): rz_total, pq_total = lax.psum((rz_part, pq_part), ('grp', 'sub'))  83.7 us
    ppermute x4, waiting for transfers between devices, shifted(): return lax.ppermute(value, axis, pairs)  74.7 us
    psum x1, waiting for transfers between devices, body(): summed = lax.psum(solved, 'grp')  65.5 us
    all_gather x1, waiting for transfers between devices, body(): group_primal = lax.all_gather(own_primal, 'sub', axis=0, tiled=True)  39.7 us
  transfers between devices with their start and end apart: 6, of which 5 were waited for; matrix products, arithmetic and copies ran while one was open for 4% of the time, Pallas kernels for 0%

commit v1 on v0

--- a/solution.py
+++ b/solution.py
@@ -38,7 +38,8 @@
     group_primal = lax.all_gather(own_primal, "sub", axis=0, tiled=True)
     my_rows = lax.dynamic_slice_in_dim(coarse_inverse, position * primal_count, primal_count, 0)
     solved = jnp.dot(my_rows, group_primal, precision=highest)
-    summed = lax.psum(solved, "grp")
+    aux = lax.all_gather(solved, "grp")
+    summed = jnp.sum(aux, 0)
     correction = solved + summed / lax.axis_size("grp")
     scattered = lax.dot_general(onehot, correction, (((0,), (0,)), ((), ())), precision=highest)
     direction = 0.5 * local_part + scattered

time: 311 us -> 260 us (0.84)
  waiting for transfers between devices: 180 us -> 120 us
  blocking collectives: 83.7 us -> 93.1 us
    psum x1 -> x0, waiting for transfers between devices: 65.5 us -> none  [body(): summed = lax.psum(solved, 'grp')]
    all_gather x0 -> x1, blocking collectives: none -> 16.6 us  [body(): aux = lax.all_gather(solved, 'grp')]
    psum x1, blocking collectives: 83.7 us -> 76.4 us  [body(): rz_total, pq_total = lax.psum((rz_part, pq_part), ('grp', 'sub'))]
    ppermute x4, waiting for transfers between devices: 74.7 us -> 80.5 us  [shifted(): return lax.ppermute(value, axis, pairs)]
  transfers between devices with their start and end apart: 6 -> 5, of which waited for: 5 -> 4; matrix products, arithmetic and copies ran while one was open for 4% -> 5% of each run, Pallas kernels for 0% -> 0%
where the time goes in v1:
time: 260 us; the launch traced here: 259 us
  waiting for transfers between devices  120 us (46%)
  blocking collectives  93.1 us (36%)
  between operations  14.2 us (5%)
  matrix products  13.7 us (5%)
  other arithmetic  7.55 us (3%)
  starting transfers between devices  6.83 us (3%)
  local copies, waits for them, and re-layouts  3.7 us (1%)
    ppermute x4, waiting for transfers between devices, shifted(): return lax.ppermute(value, axis, pairs)  80.5 us
    psum x1, blocking collectives, body(): rz_total, pq_total = lax.psum((rz_part, pq_part), ('grp', 'sub'))  76.4 us
    all_gather x1, waiting for transfers between devices, body(): group_primal = lax.all_gather(own_primal, 'sub', axis=0, tiled=True)  39.7 us
    all_gather x1, blocking collectives, body(): aux = lax.all_gather(solved, 'grp')  16.6 us
    ppermute x4, starting transfers between devices, shifted(): return lax.ppermute(value, axis, pairs)  6.79 us
    dot_general x1, matrix products, transposed(): lax.dot_general(matrix, operand, (((0,), (0,)), ((), ())), preferred_elem...  5.26 us
  transfers between devices with their start and end apart: 5, of which 4 were waited for; matrix products, arithmetic and copies ran while one was open for 5% of the time, Pallas kernels for 0%

profile of v1, /device:TPU:1, one launch (start us, length us, event | category | flops | bytes accessed | tf_op | source)
XLA Modules:
  0.0 259.2 jit_solution(15024850295529538025)
XLA Ops:
  7.2 3.1 %fusion.21 = f32[8,2048]{1,0:T(8,128)} fusion(f32[256,2048]{1,0:T(8,128)} %param.7, s32[8]{0:T(128)} %bitcast.18), kind=kOutput, calls=%fused_computation.31 | convolution fusion | flops 50333696 | bytes 2162720 | tf_op jit(solution)/shard_map/dot_general | solution.py:36
  10.4 0.1 convert_element_type.39
  10.6 1.0 copy-done.6
  11.5 2.5 collective-permute-start
  14.0 30.4 %collective-permute-done = bf16[256,2048]{1,0:T(8,128)(2,1)} collective-permute-done((bf16[256,2048]{1,0:T(8,128)(2,1)S(1)}, bf16[256,2048]{1,0:T(8,128)(2,1)}, u32[]{:S(2)}, u32[]{:S(2)}) %collective-permute-start) | collective-permute-done | bytes 1048608 | tf_op jit(solution)/shard_map/ppermute | solution.py:10
  44.4 5.3 %fusion = bf16[512,2048]{1,0:T(8,128)(2,1)} fusion(bf16[512,512]{1,0:T(8,128)(2,1)S(1)} %copy-done, bf16[256,2048]{1,0:T(8,128)(2,1)} %copy-done.6, bf16[256,2048]{1,0:T(8,128)(2,1)} %collective-permute-done), kind=kOutput, calls=%fused_computation.6 | convolution fusion | flops 2153775104 | bytes 4718592 | tf_op jit(solution)/shard_map/dot_general | solution.py:14
  49.7 2.3 slice.17
  52.0 1.3 collective-permute-start.1
  53.3 39.7 %all-gather.3.cloned.1.call-done = f32[256,2048]{1,0:T(8,128)} async-done(((f32[8,2048]{1,0:T(8,128)}), f32[256,2048]{1,0:T(8,128)}) %all-gather.3.cloned.1.call-update) | async-done | bytes 2097168 | tf_op jit(solution)/shard_map/all_gather | solution.py:38
  93.0 2.7 %fusion.19 = f32[8,2048]{1,0:T(8,128)S(1)} fusion(f32[256,2048]{1,0:T(8,128)} %all-gather.3.cloned.1.call-done, f32[256,256]{1,0:T(8,128)} %param.10, s32[]{:T(128)S(6)} %select_n.3), kind=kOutput, calls=%fused_computation.28 | convolution fusion | flops 50331648 | bytes 2170884 | tf_op jit(solution)/shard_map/dot_general | solution.py:40
  95.7 16.6 %all-gather = f32[64,2048]{1,0:T(8,128)S(1)} all-gather(f32[8,2048]{1,0:T(8,128)S(1)} %fusion.19), channel_id=2, replica_groups=mesh['grp'=8,'sub'=32] {'grp'}, dimensions={0}, use_global_device_ids=true | all-gather | bytes 589824 | tf_op jit(solution)/shard_map/all_gather | solution.py:41
  112.4 1.1 fusion.15
  113.5 1.9 multiply_reduce_fusion
  115.4 1.8 collective-permute-start.2
  117.2 27.5 %collective-permute-done.2 = bf16[256,2048]{1,0:T(8,128)(2,1)S(1)} collective-permute-done((bf16[256,2048]{1,0:T(8,128)(2,1)S(1)}, bf16[256,2048]{1,0:T(8,128)(2,1)S(1)}, u32[]{:S(2)}, u32[]{:S(2)}) %collective-permute-start.2) | collective-permute-done | bytes 1048608 | tf_op jit(solution)/shard_map/ppermute | solution.py:10
  144.7 1.3 fusion.1
  146.0 0.1 slice.19
  146.1 1.3 collective-permute-start.3
  147.4 0.2 fusion.13
  147.6 22.6 %collective-permute-done.3 = bf16[256,2048]{1,0:T(8,128)(2,1)S(1)} collective-permute-done((bf16[256,2048]{1,0:T(8,128)(2,1)S(1)}, bf16[256,2048]{1,0:T(8,128)(2,1)S(1)}, u32[]{:S(2)}, u32[]{:S(2)}) %collective-permute-start.3) | collective-permute-done | bytes 1048608 | tf_op jit(solution)/shard_map/ppermute | solution.py:10
  170.2 0.7 fusion.3
  170.9 0.3 copy-done.4
  171.2 76.4 %all-reduce = (f32[2048]{0:T(1024)S(1)}, f32[2048]{0:T(1024)S(1)}) all-reduce(f32[2048]{0:T(1024)S(1)} %get-tuple-element.4, f32[2048]{0:T(1024)S(1)} %fusion.3), channel_id=1, replica_groups=mesh['grp'=8,'sub'=32] {'grp','sub'}, use_global_device_ids=true, to_apply=%region_2.0 | all-reduce | flops 4096 | bytes 32768 | tf_op jit(solution)/shard_map/psum | solution.py:64
  247.6 4.8 %multiply_subtract_fusion = (f32[256,2048]{1,0:T(8,128)}, f32[256,2048]{1,0:T(8,128)}) fusion(f32[256,2048]{1,0:T(8,128)S(1)} %copy-done.1, bf16[256,2048]{1,0:T(8,128)(2,1)} %copy-done.2, bf16[256,2048]{1,0:T(8,128)(2,1)} %copy-done.4, f32[2048]{0:T(1024)S(1)} %div.11, f32[256]{0:T(256)S(1)} %bitcast.17, bf16[512,2048]{1,0:T(8,128)(2,1)} %copy-done.3), kind=kLoop, calls=%fused_computation.16 | loop fusion | flops 4718592 | bytes 9446400 | tf_op jit(solution)/shard_map/sub | solution.py:66
  (25 shorter events, 0.1 us)
Async XLA Ops:
  7.2 37.3 %copy-start = (bf16[512,512]{1,0:T(8,128)(2,1)S(1)}, bf16[512,512]{1,0:T(8,128)(2,1)}, u32[]{:S(2)}) copy-start(bf16[512,512]{1,0:T(8,128)(2,1)} %param.9) | copy-start | bytes 1572868
  7.2 3.2 %copy-start.1 = (f32[256,2048]{1,0:T(8,128)S(1)}, f32[256,2048]{1,0:T(8,128)}, u32[]{:S(2)}) copy-start(f32[256,2048]{1,0:T(8,128)} %param.7) | copy-start | bytes 6291460
  7.2 85.8 %all-gather.3.cloned.1.call-start = ((), (), s32[]{:S(2)}) async-start(), calls=%async_computation | async-start | bytes 2162688 | tf_op jit(solution)/shard_map/all_gather | solution.py:38
  10.6 1.0 copy-start.6
  11.5 32.9 %collective-permute-start = (bf16[256,2048]{1,0:T(8,128)(2,1)S(1)}, bf16[256,2048]{1,0:T(8,128)(2,1)}, u32[]{:S(2)}, u32[]{:S(2)}) collective-permute-start(bf16[256,2048]{1,0:T(8,128)(2,1)S(1)} %convert_element_type.39), channel_id=1, source_target_pairs={{0,1},{1,2},{2,3},{3,4},{4,5},{5,6},{6,7},{7,8},{8,9},{9,10},{10,1... | collective-permute-start | bytes 3145736 | tf_op jit(solution)/shard_map/ppermute | solution.py:10
  52.0 60.4 %copy-start.7 = (s32[1,8]{1,0:T(1,128)S(1)}, s32[1,8]{1,0:T(1,128)}, u32[]{:S(2)}) copy-start(s32[1,8]{1,0:T(1,128)} %param.11) | copy-start | bytes 100
  52.0 61.5 %collective-permute-start.1 = (bf16[256,2048]{1,0:T(8,128)(2,1)}, bf16[256,2048]{1,0:T(8,128)(2,1)}, u32[]{:S(2)}, u32[]{:S(2)}) collective-permute-start(bf16[256,2048]{1,0:T(8,128)(2,1)} %slice.17), channel_id=1, source_target_pairs={{0,31},{1,0},{2,1},{3,2},{4,3},{5,4},{6,5},{7,6},{8,7},{9,8},{10,9... | collective-permute-start | bytes 3145736 | tf_op jit(solution)/shard_map/ppermute | solution.py:10
  95.7 17.8 %copy-start.5 = (bf16[512,2048]{1,0:T(8,128)(2,1)S(1)}, bf16[512,2048]{1,0:T(8,128)(2,1)}, u32[]{:S(2)}) copy-start(bf16[512,2048]{1,0:T(8,128)(2,1)} %fusion) | copy-start | bytes 6291460
  113.5 31.2 %copy-start.8 = (bf16[512,512]{1,0:T(8,128)(2,1)S(1)}, bf16[512,512]{1,0:T(8,128)(2,1)}, u32[]{:S(2)}) copy-start(bf16[512,512]{1,0:T(8,128)(2,1)} %param.8) | copy-start | bytes 1572868
  115.4 54.7 %copy-start.2 = (bf16[256,2048]{1,0:T(8,128)(2,1)}, bf16[256,2048]{1,0:T(8,128)(2,1)S(1)}, u32[]{:S(2)}) copy-start(bf16[256,2048]{1,0:T(8,128)(2,1)S(1)} %get-tuple-element.5) | copy-start | bytes 3145732
  115.4 29.3 %collective-permute-start.2 = (bf16[256,2048]{1,0:T(8,128)(2,1)S(1)}, bf16[256,2048]{1,0:T(8,128)(2,1)S(1)}, u32[]{:S(2)}, u32[]{:S(2)}) collective-permute-start(bf16[256,2048]{1,0:T(8,128)(2,1)S(1)} %get-tuple-element.5), channel_id=1, source_target_pairs={{0,1},{1,2},{2,3},{3,4},{4,5},{5,6},{6,7},{7,8},{8,9},{9,10},{10,1... | collective-permute-start | bytes 3145736 | tf_op jit(solution)/shard_map/ppermute | solution.py:10
  146.0 24.9 %copy-start.3 = (bf16[512,2048]{1,0:T(8,128)(2,1)}, bf16[512,2048]{1,0:T(8,128)(2,1)S(1)}, u32[]{:S(2)}) copy-start(bf16[512,2048]{1,0:T(8,128)(2,1)S(1)} %fusion.1) | copy-start | bytes 6291460
  146.0 1.4 copy-start.9
  146.0 1.4 copy-start.10
  146.1 24.1 %collective-permute-start.3 = (bf16[256,2048]{1,0:T(8,128)(2,1)S(1)}, bf16[256,2048]{1,0:T(8,128)(2,1)S(1)}, u32[]{:S(2)}, u32[]{:S(2)}) collective-permute-start(bf16[256,2048]{1,0:T(8,128)(2,1)S(1)} %slice.19), channel_id=1, source_target_pairs={{0,31},{1,0},{2,1},{3,2},{4,3},{5,4},{6,5},{7,6},{8,7},{9,8},{10,9... | collective-permute-start | bytes 3145736 | tf_op jit(solution)/shard_map/ppermute | solution.py:10
  170.2 1.0 copy-start.4
Sparse Core Ops, SparseCore 0:
  10.6 82.3 all-gather.2
